TPU v7x, 32 devices: a whole 2x2x4 slice. The times are simulated.
32 devices in a mesh: wide: 8 (over y, x, core), narrow: 4 (over z).
Axes of the slice: x: 2, y: 2, z: 4, core: 2. Of those that a mesh axis runs over, the one named last changes fastest.
Arguments:
- states: bfloat16 [16384, 1024], P(('wide', 'narrow')), may hold values from -6 to 6
- applied: bfloat16 [16384, 1024], P(('wide', 'narrow')), may hold values from -6 to 6
- rotation: bfloat16 [2, 1024, 256], P(None, 'wide', 'narrow'), may hold values from -0.1875 to 0.1875
- ritz: float32 [2, 256], replicated, may hold values from 0.5 to 4
- potential: float32 [16384], P(('wide', 'narrow')), may hold values from 0.5 to 8
Outputs:
- rotated: bfloat16 [16384, 2, 256], P(('wide', 'narrow'))
- correction: bfloat16 [16384, 2, 256], P(('wide', 'narrow'))
- margin: float32 [2, 1024, 256], P(None, 'wide', 'narrow')
All inputs are finite; a program needn't handle non-finite values.
Results may differ from a plain program's by a relative error of at most 0.0095.
Values may be sent and summed in bfloat16 or wider, within the bound.
A program may use at most 64 MiB of HBM per device.

v0:
```python
import math
import jax
import jax.numpy as jnp
from jax import lax
from jax.sharding import PartitionSpec as P


def per_device(states, applied, rotation, ritz, potential):
    row_count = states.shape[0]
    total_rows = row_count * lax.axis_size("wide") * lax.axis_size("narrow")
    factor = 1.0 / math.sqrt(total_rows)
    contract = (((0,), (0,)), ((), ()))
    rotated_list = []
    correction_list = []
    margin_list = []
    for window in range(rotation.shape[0]):
        q_local = rotation[window]
        q_tall = lax.all_gather(q_local, "wide", axis=0, tiled=True)
        q_full = lax.all_gather(q_tall, "narrow", axis=1, tiled=True)
        plain = jnp.dot(states, q_full, preferred_element_type=jnp.float32)
        mapped = jnp.dot(applied, q_full, preferred_element_type=jnp.float32)
        eigen_values = ritz[window]
        residual = mapped - plain * eigen_values[None, :]
        fixed = (residual / (potential[:, None] + eigen_values[None, :])).astype(jnp.bfloat16)
        partial_value = lax.psum_scatter(
            lax.dot_general(states, fixed, contract, preferred_element_type=jnp.float32).astype(
                jnp.bfloat16
            ),
            "wide",
            scatter_dimension=0,
            tiled=True,
        )
        summed = lax.psum_scatter(partial_value, "narrow", scatter_dimension=1, tiled=True).astype(
            jnp.float32
        )
        rotated_list.append(plain.astype(jnp.bfloat16))
        correction_list.append(fixed)
        margin_list.append(summed * factor)
    return (
        jnp.stack(rotated_list, axis=1),
        jnp.stack(correction_list, axis=1),
        jnp.stack(margin_list, axis=0),
    )


def solution(mesh):
    placed = (
        P(("wide", "narrow"), None),
        P(("wide", "narrow"), None),
        P(None, "wide", "narrow"),
        P(),
        P(("wide", "narrow")),
    )
    return jax.shard_map(
        per_device,
        mesh=mesh,
        in_specs=placed,
        out_specs=(
            P(("wide", "narrow"), None, None),
            P(("wide", "narrow"), None, None),
            P(None, "wide", "narrow"),
        ),
        check_vma=False,
    )
```

profile of v0, /device:TPU:0, one launch (start us, length us, event | category | flops | bytes accessed | tf_op | source)
XLA Modules:
  0.0 160.5 jit_solution(8119105058409660867)
XLA Ops:
  7.2 0.0 copy-start
  7.2 0.0 reduce-scatter.15.cloned.1.call-start
  7.2 0.8 fusion.13
  8.0 0.7 fusion.12
  8.7 10.5 %all-gather.2 = bf16[1,1024,64]{1,2,0:T(8,128)(2,1)S(1)} all-gather(bf16[1,128,64]{1,2,0:T(8,128)(2,1)S(1)} %get-tuple-element.10), channel_id=4, replica_groups=mesh['wide'=8,'narrow'=4] {'wide'}, dimensions={1}, use_global_device_ids=true | all-gather | bytes 147456 | tf_op jit(solution)/shard_map/all_gather | solution.py:18
  19.3 16.3 %all-gather.3 = bf16[1,1024,256]{1,2,0:T(8,128)(2,1)S(1)} all-gather(bf16[1,1024,64]{1,2,0:T(8,128)(2,1)S(1)} %all-gather.2), channel_id=5, replica_groups=mesh['wide'=8,'narrow'=4] {'narrow'}, dimensions={2}, use_global_device_ids=true | all-gather | bytes 655360 | tf_op jit(solution)/shard_map/all_gather | solution.py:19
  35.6 0.0 copy-done
  35.6 0.0 copy-start.1
  35.6 0.5 fusion.7
  36.1 0.0 copy-start.3
  36.1 0.7 copy-done.1
  36.8 0.0 copy-done.3
  36.8 0.5 fusion.4
  37.3 0.5 fusion.3
  37.8 1.0 copy.14
  38.8 0.0 reduce-scatter.15.cloned.1.call-update
  38.8 0.0 reduce-scatter.13.cloned.1.call-start
  38.9 9.0 %all-gather = bf16[1,1024,64]{1,2,0:T(8,128)(2,1)S(1)} all-gather(bf16[1,128,64]{1,2,0:T(8,128)(2,1)S(1)} %get-tuple-element.9), channel_id=2, replica_groups=mesh['wide'=8,'narrow'=4] {'wide'}, dimensions={1}, use_global_device_ids=true | all-gather | bytes 147456 | tf_op jit(solution)/shard_map/all_gather | solution.py:18
  47.9 16.6 %all-gather.1 = bf16[1,1024,256]{1,2,0:T(8,128)(2,1)S(1)} all-gather(bf16[1,1024,64]{1,2,0:T(8,128)(2,1)S(1)} %all-gather), channel_id=3, replica_groups=mesh['wide'=8,'narrow'=4] {'narrow'}, dimensions={2}, use_global_device_ids=true | all-gather | bytes 655360 | tf_op jit(solution)/shard_map/all_gather | solution.py:19
  64.5 0.0 copy-start.2
  64.5 0.5 fusion.10
  65.0 0.7 copy-done.2
  65.7 0.5 fusion.5
  66.2 0.5 fusion.2
  66.6 1.0 copy.12
  67.6 0.0 reduce-scatter.13.cloned.1.call-update
  67.7 0.0 reduce-scatter.11.cloned.1.call-start
  67.8 5.8 %reduce-scatter.15.cloned.1.call-done = bf16[128,256]{1,0:T(8,128)(2,1)} async-done(((bf16[1024,256]{1,0:T(8,128)(2,1)}), bf16[128,256]{1,0:T(8,128)(2,1)}) %reduce-scatter.15.cloned.1.call-update) | async-done | bytes 65552
  73.6 1.6 copy.15
  75.2 0.0 reduce-scatter.11.cloned.1.call-update
  75.2 0.0 reduce-scatter.9.cloned.1.call-start
  75.3 0.1 pad_maximum_fusion
  75.3 1.3 copy.10
  76.7 0.1 pad_maximum_fusion.1
  76.7 1.3 copy.11
  78.0 32.8 %reduce-scatter.13.cloned.1.call-done = bf16[128,256]{1,0:T(8,128)(2,1)} async-done(((bf16[1024,256]{1,0:T(8,128)(2,1)}), bf16[128,256]{1,0:T(8,128)(2,1)}) %reduce-scatter.13.cloned.1.call-update) | async-done | bytes 65552
  110.9 1.6 copy.13
  112.4 0.0 reduce-scatter.9.cloned.1.call-update
  112.5 20.6 %reduce-scatter.11.cloned.1.call-done = bf16[128,64]{0,1:T(8,128)(2,1)} async-done(((bf16[128,256]{0,1:T(8,128)(2,1)}), bf16[128,64]{0,1:T(8,128)(2,1)}) %reduce-scatter.11.cloned.1.call-update) | async-done | bytes 16400 | tf_op jit(solution)/shard_map/reduce_scatter | solution.py:33
  133.0 0.7 multiply_bitcast_fusion
  133.7 18.9 %reduce-scatter.9.cloned.1.call-done = bf16[128,64]{0,1:T(8,128)(2,1)} async-done(((bf16[128,256]{0,1:T(8,128)(2,1)}), bf16[128,64]{0,1:T(8,128)(2,1)}) %reduce-scatter.9.cloned.1.call-update) | async-done | bytes 16400 | tf_op jit(solution)/shard_map/reduce_scatter | solution.py:33
  152.6 0.7 multiply_bitcast_fusion.1
  153.3 0.6 pad_maximum_fusion.2
  (2 shorter events, 0.1 us)
Async XLA Ops:
  7.2 28.4 %copy-start = (bf16[512,1024]{1,0:T(8,128)(2,1)S(1)}, bf16[512,1024]{1,0:T(8,128)(2,1)}, u32[]{:S(2)}) copy-start(bf16[512,1024]{1,0:T(8,128)(2,1)} %param.5) | copy-start | bytes 3145732
  7.2 66.4 %reduce-scatter.15.cloned.1.call-start = ((), (), s32[]{:S(2)}) async-start(), calls=%async_computation.7 | async-start | bytes 589824
  35.6 1.2 copy-start.1
  36.1 0.7 copy-start.3
  38.8 72.1 %reduce-scatter.13.cloned.1.call-start = ((), (), s32[]{:S(2)}) async-start(), calls=%async_computation.6 | async-start | bytes 589824
  64.5 1.2 copy-start.2
  67.7 65.3 %reduce-scatter.11.cloned.1.call-start = ((), (), s32[]{:S(2)}) async-start(), calls=%async_computation.5 | async-start | bytes 81920 | tf_op jit(solution)/shard_map/reduce_scatter | solution.py:33
  75.2 77.4 %reduce-scatter.9.cloned.1.call-start = ((), (), s32[]{:S(2)}) async-start(), calls=%async_computation.4 | async-start | bytes 81920 | tf_op jit(solution)/shard_map/reduce_scatter | solution.py:33
Sparse Core Ops, SparseCore 0:
  38.9 34.6 reduce-scatter.14
  76.7 34.1 reduce-scatter.12
  113.7 19.2 reduce-scatter.10
  135.1 17.4 reduce-scatter.8
where the time goes:
time: 161 us; the launch traced here: 160 us
  waiting for transfers between devices  78.1 us (49%)
  blocking collectives  52.5 us (33%)
  between operations  13.9 us (9%)
  local copies, waits for them, and re-layouts  10.8 us (7%)
  matrix products  2.82 us (2%)
  other arithmetic  2.24 us (1%)
    reduce_scatter x2, waiting for transfers between devices, per_device(): lax.psum_scatter(partial_value, 'narrow', scatter_dimension=1, tiled=True)  39.4 us
    unnamed x6, waiting for transfers between devices  38.7 us
    all_gather x2, blocking collectives, per_device(): q_full = lax.all_gather(q_tall, 'narrow', axis=1, tiled=True)  32.9 us
    all_gather x2, blocking collectives, per_device(): q_tall = lax.all_gather(q_local, 'wide', axis=0, tiled=True)  19.6 us
    unnamed x14, local copies, waits for them, and re-layouts  9.3 us
  transfers between devices with their start and end apart: 4, of which 4 were waited for; matrix products, arithmetic and copies ran while one was open for 6% of the time, Pallas kernels for 0%

commit v1 on v0

--- a/solution.py
+++ b/solution.py
@@ -15,7 +15,14 @@
     margin_list = []
     for window in range(rotation.shape[0]):
         q_local = rotation[window]
-        q_tall = lax.all_gather(q_local, "wide", axis=0, tiled=True)
+        ring = [q_local]
+        for hop in range(7):
+            ring.append(lax.ppermute(ring[-1], "wide", [(dev, (dev + 1) % 8) for dev in range(8)]))
+        q_tall = jnp.roll(
+            jnp.concatenate(ring[::-1], axis=0),
+            (lax.axis_index("wide") + 1) * ring[0].shape[0],
+            axis=0,
+        )
         q_full = lax.all_gather(q_tall, "narrow", axis=1, tiled=True)
         plain = jnp.dot(states, q_full, preferred_element_type=jnp.float32)
         mapped = jnp.dot(applied, q_full, preferred_element_type=jnp.float32)

time: 161 us -> 195 us (1.21)
  waiting for transfers between devices: 78.1 us -> 125 us
  blocking collectives: 52.5 us -> 33.2 us
  starting transfers between devices: 0.16 us -> 4.96 us
    ppermute x0 -> x14, waiting for transfers between devices: none -> 24.4 us  [per_device(): lax.ppermute(ring[-1], 'wide', [(dev, (dev + 1) % 8) for dev in range(8)])]
    unnamed x6, waiting for transfers between devices: 38.7 us -> 61.6 us
    all_gather x2 -> x0, blocking collectives: 19.6 us -> none  [per_device(): q_tall = lax.all_gather(q_local, 'wide', axis=0, tiled=True)]
    ppermute x0 -> x14, starting transfers between devices: none -> 4.79 us  [per_device(): lax.ppermute(ring[-1], 'wide', [(dev, (dev + 1) % 8) for dev in range(8)])]
    unnamed x14 -> x36, local copies, waits for them, and re-layouts: 9.3 us -> 10.4 us
  transfers between devices with their start and end apart: 4 -> 18, of which waited for: 4 -> 18; matrix products, arithmetic and copies ran while one was open for 6% -> 4% of each run, Pallas kernels for 0% -> 0%
where the time goes in v1:
time: 195 us; the launch traced here: 194 us
  waiting for transfers between devices  125 us (64%)
  blocking collectives  33.2 us (17%)
  between operations  14 us (7%)
  local copies, waits for them, and re-layouts  11.2 us (6%)
  starting transfers between devices  4.96 us (3%)
  matrix products  2.77 us (1%)
  other arithmetic  2.43 us (1%)
    unnamed x6, waiting for transfers between devices  61.6 us
    reduce_scatter x2, waiting for transfers between devices, per_device(): lax.psum_scatter(partial_value, 'narrow', scatter_dimension=1, tiled=True)  39.4 us
    all_gather x2, blocking collectives, per_device(): q_full = lax.all_gather(q_tall, 'narrow', axis=1, tiled=True)  33.2 us
    ppermute x14, waiting for transfers between devices, per_device(): lax.ppermute(ring[-1], 'wide', [(dev, (dev + 1) % 8) for dev in range(8)])  24.4 us
    unnamed x36, local copies, waits for them, and re-layouts  10.4 us
    ppermute x14, starting transfers between devices, per_device(): lax.ppermute(ring[-1], 'wide', [(dev, (dev + 1) % 8) for dev in range(8)])  4.79 us
  transfers between devices with their start and end apart: 18, of which 18 were waited for; matrix products, arithmetic and copies ran while one was open for 4% of the time, Pallas kernels for 0%

profile of v1, /device:TPU:0, one launch (start us, length us, event | category | flops | bytes accessed | tf_op | source)
XLA Modules:
  0.0 194.1 jit_solution(587853179236058857)
XLA Ops:
  7.2 0.0 copy-start
  7.2 0.0 reduce-scatter.15.cloned.1.call-start
  7.2 0.8 slice_bitcast_fusion.1
  8.0 0.5 collective-permute-start.7
  8.5 2.6 %collective-permute-start = (bf16[128,64]{0,1:T(8,128)(2,1)S(1)}, bf16[128,64]{0,1:T(8,128)(2,1)S(1)}, u32[]{:S(2)}, u32[]{:S(2)}) collective-permute-start(bf16[128,64]{0,1:T(8,128)(2,1)S(1)} %get-tuple-element.12), channel_id=1, source_target_pairs={{0,4},{4,8},{8,12},{12,16},{16,20},{20,24},{24,28},{28,0},{1,5},{5... | collective-permute-start | bytes 49160 | tf_op jit(solution)/shard_map/ppermute | solution.py:20
  11.1 1.7 collective-permute-done.7
  12.8 0.2 collective-permute-done
  13.0 1.3 collective-permute-start.1
  14.3 2.6 %collective-permute-done.8 = bf16[128,64]{0,1:T(8,128)(2,1)S(1)} collective-permute-done((bf16[128,64]{0,1:T(8,128)(2,1)S(1)}, bf16[128,64]{0,1:T(8,128)(2,1)S(1)}, u32[]{:S(2)}, u32[]{:S(2)}) %collective-permute-start.8) | collective-permute-done | bytes 16416 | tf_op jit(solution)/shard_map/ppermute | solution.py:20
  16.9 0.0 collective-permute-start.9
  16.9 0.2 collective-permute-done.1
  17.1 0.4 collective-permute-start.2
  17.5 3.5 %collective-permute-done.9 = bf16[128,64]{0,1:T(8,128)(2,1)S(1)} collective-permute-done((bf16[128,64]{0,1:T(8,128)(2,1)S(1)}, bf16[128,64]{0,1:T(8,128)(2,1)S(1)}, u32[]{:S(2)}, u32[]{:S(2)}) %collective-permute-start.9) | collective-permute-done | bytes 16416 | tf_op jit(solution)/shard_map/ppermute | solution.py:20
  21.0 0.0 collective-permute-start.10
  21.0 0.2 collective-permute-done.2
  21.1 3.9 %collective-permute-done.10 = bf16[128,64]{0,1:T(8,128)(2,1)S(1)} collective-permute-done((bf16[128,64]{0,1:T(8,128)(2,1)S(1)}, bf16[128,64]{0,1:T(8,128)(2,1)S(1)}, u32[]{:S(2)}, u32[]{:S(2)}) %collective-permute-start.10) | collective-permute-done | bytes 16416 | tf_op jit(solution)/shard_map/ppermute | solution.py:20
  25.0 0.2 collective-permute-done.3
  25.2 0.0 collective-permute-start.4
  25.2 3.9 %collective-permute-done.11 = bf16[128,64]{0,1:T(8,128)(2,1)S(1)} collective-permute-done((bf16[128,64]{0,1:T(8,128)(2,1)S(1)}, bf16[128,64]{0,1:T(8,128)(2,1)S(1)}, u32[]{:S(2)}, u32[]{:S(2)}) %collective-permute-start.11) | collective-permute-done | bytes 16416 | tf_op jit(solution)/shard_map/ppermute | solution.py:20
  29.1 0.2 collective-permute-done.4
  29.3 0.0 collective-permute-start.5
  29.3 3.9 %collective-permute-done.12 = bf16[128,64]{0,1:T(8,128)(2,1)S(1)} collective-permute-done((bf16[128,64]{0,1:T(8,128)(2,1)S(1)}, bf16[128,64]{0,1:T(8,128)(2,1)S(1)}, u32[]{:S(2)}, u32[]{:S(2)}) %collective-permute-start.12) | collective-permute-done | bytes 16416 | tf_op jit(solution)/shard_map/ppermute | solution.py:20
  33.2 0.1 collective-permute-done.5
  33.3 3.9 %collective-permute-done.13 = bf16[128,64]{0,1:T(8,128)(2,1)S(1)} collective-permute-done((bf16[128,64]{0,1:T(8,128)(2,1)S(1)}, bf16[128,64]{0,1:T(8,128)(2,1)S(1)}, u32[]{:S(2)}, u32[]{:S(2)}) %collective-permute-start.13) | collective-permute-done | bytes 16416 | tf_op jit(solution)/shard_map/ppermute | solution.py:20
  37.3 0.1 collective-permute-done.6
  37.4 0.0 copy-start.3
  37.5 0.7 copy-done.3
  38.2 0.1 fusion.9
  38.3 0.1 fusion.8
  38.4 17.2 %all_gather.7 = bf16[1024,256]{0,1:T(8,128)(2,1)S(1)} all-gather(bf16[1024,64]{0,1:T(8,128)(2,1)S(1)} %fusion.8), channel_id=1, replica_groups=mesh['wide'=8,'narrow'=4] {'narrow'}, dimensions={1}, use_global_device_ids=true | all-gather | bytes 655360 | tf_op jit(solution)/shard_map/all_gather | solution.py:26
  55.6 16.1 %all_gather.6 = bf16[1024,256]{0,1:T(8,128)(2,1)S(1)} all-gather(bf16[1024,64]{0,1:T(8,128)(2,1)S(1)} %fusion.9), channel_id=1, replica_groups=mesh['wide'=8,'narrow'=4] {'narrow'}, dimensions={1}, use_global_device_ids=true | all-gather | bytes 655360 | tf_op jit(solution)/shard_map/all_gather | solution.py:26
  71.7 0.5 fusion.12
  72.1 0.0 copy-start.7
  72.2 0.7 copy-done.5
  72.9 0.5 fusion.6
  73.4 0.4 fusion.5
  73.8 1.0 copy.14
  74.8 0.0 reduce-scatter.15.cloned.1.call-update
  74.8 0.0 reduce-scatter.13.cloned.1.call-start
  74.9 0.0 copy-start.6
  74.9 0.5 fusion.11
  75.4 0.7 copy-done.6
  76.1 0.5 fusion.7
  76.6 0.7 copy-done.1
  77.3 0.4 fusion.4
  77.7 1.0 copy.12
  78.8 0.0 reduce-scatter.13.cloned.1.call-update
  78.8 0.0 reduce-scatter.11.cloned.1.call-start
  78.9 28.3 %reduce-scatter.15.cloned.1.call-done = bf16[128,256]{1,0:T(8,128)(2,1)} async-done(((bf16[1024,256]{1,0:T(8,128)(2,1)}), bf16[128,256]{1,0:T(8,128)(2,1)}) %reduce-scatter.15.cloned.1.call-update) | async-done | bytes 65552
  107.2 1.6 copy.15
  108.8 0.0 reduce-scatter.11.cloned.1.call-update
  108.8 0.0 reduce-scatter.9.cloned.1.call-start
  108.8 0.1 pad_maximum_fusion
  108.9 1.1 copy.10
  110.0 0.1 pad_maximum_fusion.1
  110.1 1.1 copy.11
  111.2 33.3 %reduce-scatter.13.cloned.1.call-done = bf16[128,256]{1,0:T(8,128)(2,1)} async-done(((bf16[1024,256]{1,0:T(8,128)(2,1)}), bf16[128,256]{1,0:T(8,128)(2,1)}) %reduce-scatter.13.cloned.1.call-update) | async-done | bytes 65552
  144.4 1.6 copy.13
  146.0 0.0 reduce-scatter.9.cloned.1.call-update
  146.0 20.6 %reduce-scatter.11.cloned.1.call-done = bf16[128,64]{0,1:T(8,128)(2,1)} async-done(((bf16[128,256]{0,1:T(8,128)(2,1)}), bf16[128,64]{0,1:T(8,128)(2,1)}) %reduce-scatter.11.cloned.1.call-update) | async-done | bytes 16400 | tf_op jit(solution)/shard_map/reduce_scatter | solution.py:40
  166.6 0.7 multiply_bitcast_fusion
  167.3 18.9 %reduce-scatter.9.cloned.1.call-done = bf16[128,64]{0,1:T(8,128)(2,1)} async-done(((bf16[128,256]{0,1:T(8,128)(2,1)}), bf16[128,64]{0,1:T(8,128)(2,1)}) %reduce-scatter.9.cloned.1.call-update) | async-done | bytes 16400 | tf_op jit(solution)/shard_map/reduce_scatter | solution.py:40
  186.2 0.7 multiply_bitcast_fusion.1
  186.9 0.6 pad_maximum_fusion.2
  (32 shorter events, 0.2 us)
Async XLA Ops:
  7.2 64.5 %copy-start = (bf16[512,1024]{1,0:T(8,128)(2,1)S(1)}, bf16[512,1024]{1,0:T(8,128)(2,1)}, u32[]{:S(2)}) copy-start(bf16[512,1024]{1,0:T(8,128)(2,1)} %param.7) | copy-start | bytes 3145732
  7.2 100.0 %reduce-scatter.15.cloned.1.call-start = ((), (), s32[]{:S(2)}) async-start(), calls=%async_computation.7 | async-start | bytes 589824
  8.0 25.1 %copy-start.4 = (f32[2,256]{1,0:T(2,128)S(1)}, f32[2,256]{1,0:T(2,128)}, u32[]{:S(2)}) copy-start(f32[2,256]{1,0:T(2,128)} %param.10) | copy-start | bytes 6148
  8.0 4.8 %collective-permute-start.7 = (bf16[128,64]{0,1:T(8,128)(2,1)S(1)}, bf16[128,64]{0,1:T(8,128)(2,1)S(1)}, u32[]{:S(2)}, u32[]{:S(2)}) collective-permute-start(bf16[128,64]{0,1:T(8,128)(2,1)S(1)} %get-tuple-element.13), channel_id=1, source_target_pairs={{0,4},{4,8},{8,12},{12,16},{16,20},{20,24},{24,28},{28,0},{1,5},{5... | collective-permute-start | bytes 49160 | tf_op jit(solution)/shard_map/ppermute | solution.py:20
  8.5 4.5 %collective-permute-start = (bf16[128,64]{0,1:T(8,128)(2,1)S(1)}, bf16[128,64]{0,1:T(8,128)(2,1)S(1)}, u32[]{:S(2)}, u32[]{:S(2)}) collective-permute-start(bf16[128,64]{0,1:T(8,128)(2,1)S(1)} %get-tuple-element.12), channel_id=1, source_target_pairs={{0,4},{4,8},{8,12},{12,16},{16,20},{20,24},{24,28},{28,0},{1,5},{5... | collective-permute-start | bytes 49160 | tf_op jit(solution)/shard_map/ppermute | solution.py:20
  12.8 4.1 %collective-permute-start.8 = (bf16[128,64]{0,1:T(8,128)(2,1)S(1)}, bf16[128,64]{0,1:T(8,128)(2,1)S(1)}, u32[]{:S(2)}, u32[]{:S(2)}) collective-permute-start(bf16[128,64]{0,1:T(8,128)(2,1)S(1)} %collective-permute-done.7), channel_id=1, source_target_pairs={{0,4},{4,8},{8,12},{12,16},{16,20},{20,24},{24,28},{28,0},{1,5},{5... | collective-permute-start | bytes 49160 | tf_op jit(solution)/shard_map/ppermute | solution.py:20
  13.0 4.1 %collective-permute-start.1 = (bf16[128,64]{0,1:T(8,128)(2,1)S(1)}, bf16[128,64]{0,1:T(8,128)(2,1)S(1)}, u32[]{:S(2)}, u32[]{:S(2)}) collective-permute-start(bf16[128,64]{0,1:T(8,128)(2,1)S(1)} %collective-permute-done), channel_id=1, source_target_pairs={{0,4},{4,8},{8,12},{12,16},{16,20},{20,24},{24,28},{28,0},{1,5},{5... | collective-permute-start | bytes 49160 | tf_op jit(solution)/shard_map/ppermute | solution.py:20
  16.9 4.1 %collective-permute-start.9 = (bf16[128,64]{0,1:T(8,128)(2,1)S(1)}, bf16[128,64]{0,1:T(8,128)(2,1)S(1)}, u32[]{:S(2)}, u32[]{:S(2)}) collective-permute-start(bf16[128,64]{0,1:T(8,128)(2,1)S(1)} %collective-permute-done.8), channel_id=1, source_target_pairs={{0,4},{4,8},{8,12},{12,16},{16,20},{20,24},{24,28},{28,0},{1,5},{5... | collective-permute-start | bytes 49160 | tf_op jit(solution)/shard_map/ppermute | solution.py:20
  17.1 4.1 %collective-permute-start.2 = (bf16[128,64]{0,1:T(8,128)(2,1)S(1)}, bf16[128,64]{0,1:T(8,128)(2,1)S(1)}, u32[]{:S(2)}, u32[]{:S(2)}) collective-permute-start(bf16[128,64]{0,1:T(8,128)(2,1)S(1)} %collective-permute-done.1), channel_id=1, source_target_pairs={{0,4},{4,8},{8,12},{12,16},{16,20},{20,24},{24,28},{28,0},{1,5},{5... | collective-permute-start | bytes 49160 | tf_op jit(solution)/shard_map/ppermute | solution.py:20
  21.0 4.1 %collective-permute-start.10 = (bf16[128,64]{0,1:T(8,128)(2,1)S(1)}, bf16[128,64]{0,1:T(8,128)(2,1)S(1)}, u32[]{:S(2)}, u32[]{:S(2)}) collective-permute-start(bf16[128,64]{0,1:T(8,128)(2,1)S(1)} %collective-permute-done.9), channel_id=1, source_target_pairs={{0,4},{4,8},{8,12},{12,16},{16,20},{20,24},{24,28},{28,0},{1,5},{5... | collective-permute-start | bytes 49160 | tf_op jit(solution)/shard_map/ppermute | solution.py:20
  21.1 4.1 %collective-permute-start.3 = (bf16[128,64]{0,1:T(8,128)(2,1)S(1)}, bf16[128,64]{0,1:T(8,128)(2,1)S(1)}, u32[]{:S(2)}, u32[]{:S(2)}) collective-permute-start(bf16[128,64]{0,1:T(8,128)(2,1)S(1)} %collective-permute-done.2), channel_id=1, source_target_pairs={{0,4},{4,8},{8,12},{12,16},{16,20},{20,24},{24,28},{28,0},{1,5},{5... | collective-permute-start | bytes 49160 | tf_op jit(solution)/shard_map/ppermute | solution.py:20
  25.0 4.1 %collective-permute-start.11 = (bf16[128,64]{0,1:T(8,128)(2,1)S(1)}, bf16[128,64]{0,1:T(8,128)(2,1)S(1)}, u32[]{:S(2)}, u32[]{:S(2)}) collective-permute-start(bf16[128,64]{0,1:T(8,128)(2,1)S(1)} %collective-permute-done.10), channel_id=1, source_target_pairs={{0,4},{4,8},{8,12},{12,16},{16,20},{20,24},{24,28},{28,0},{1,5},{5... | collective-permute-start | bytes 49160 | tf_op jit(solution)/shard_map/ppermute | solution.py:20
  25.2 4.1 %collective-permute-start.4 = (bf16[128,64]{0,1:T(8,128)(2,1)S(1)}, bf16[128,64]{0,1:T(8,128)(2,1)S(1)}, u32[]{:S(2)}, u32[]{:S(2)}) collective-permute-start(bf16[128,64]{0,1:T(8,128)(2,1)S(1)} %collective-permute-done.3), channel_id=1, source_target_pairs={{0,4},{4,8},{8,12},{12,16},{16,20},{20,24},{24,28},{28,0},{1,5},{5... | collective-permute-start | bytes 49160 | tf_op jit(solution)/shard_map/ppermute | solution.py:20
  29.1 4.1 %collective-permute-start.12 = (bf16[128,64]{0,1:T(8,128)(2,1)S(1)}, bf16[128,64]{0,1:T(8,128)(2,1)S(1)}, u32[]{:S(2)}, u32[]{:S(2)}) collective-permute-start(bf16[128,64]{0,1:T(8,128)(2,1)S(1)} %collective-permute-done.11), channel_id=1, source_target_pairs={{0,4},{4,8},{8,12},{12,16},{16,20},{20,24},{24,28},{28,0},{1,5},{5... | collective-permute-start | bytes 49160 | tf_op jit(solution)/shard_map/ppermute | solution.py:20
  29.3 4.1 %collective-permute-start.5 = (bf16[128,64]{0,1:T(8,128)(2,1)S(1)}, bf16[128,64]{0,1:T(8,128)(2,1)S(1)}, u32[]{:S(2)}, u32[]{:S(2)}) collective-permute-start(bf16[128,64]{0,1:T(8,128)(2,1)S(1)} %collective-permute-done.4), channel_id=1, source_target_pairs={{0,4},{4,8},{8,12},{12,16},{16,20},{20,24},{24,28},{28,0},{1,5},{5... | collective-permute-start | bytes 49160 | tf_op jit(solution)/shard_map/ppermute | solution.py:20
  33.1 4.1 %collective-permute-start.13 = (bf16[128,64]{0,1:T(8,128)(2,1)S(1)}, bf16[128,64]{0,1:T(8,128)(2,1)S(1)}, u32[]{:S(2)}, u32[]{:S(2)}) collective-permute-start(bf16[128,64]{0,1:T(8,128)(2,1)S(1)} %collective-permute-done.12), channel_id=1, source_target_pairs={{0,4},{4,8},{8,12},{12,16},{16,20},{20,24},{24,28},{28,0},{1,5},{5... | collective-permute-start | bytes 49160 | tf_op jit(solution)/shard_map/ppermute | solution.py:20
  33.3 4.1 %collective-permute-start.6 = (bf16[128,64]{0,1:T(8,128)(2,1)S(1)}, bf16[128,64]{0,1:T(8,128)(2,1)S(1)}, u32[]{:S(2)}, u32[]{:S(2)}) collective-permute-start(bf16[128,64]{0,1:T(8,128)(2,1)S(1)} %collective-permute-done.5), channel_id=1, source_target_pairs={{0,4},{4,8},{8,12},{12,16},{16,20},{20,24},{24,28},{28,0},{1,5},{5... | collective-permute-start | bytes 49160 | tf_op jit(solution)/shard_map/ppermute | solution.py:20
  37.4 0.8 copy-start.3
  71.7 1.2 copy-start.5
  72.1 0.8 copy-start.7
  74.8 69.6 %reduce-scatter.13.cloned.1.call-start = ((), (), s32[]{:S(2)}) async-start(), calls=%async_computation.6 | async-start | bytes 589824
  74.9 1.2 copy-start.6
  76.6 0.7 copy-start.1
  78.8 87.8 %reduce-scatter.11.cloned.1.call-start = ((), (), s32[]{:S(2)}) async-start(), calls=%async_computation.5 | async-start | bytes 81920 | tf_op jit(solution)/shard_map/reduce_scatter | solution.py:40
  108.8 77.4 %reduce-scatter.9.cloned.1.call-start = ((), (), s32[]{:S(2)}) async-start(), calls=%async_computation.4 | async-start | bytes 81920 | tf_op jit(solution)/shard_map/reduce_scatter | solution.py:40
  108.9 1.1 copy-start.2
Sparse Core Ops, SparseCore 0:
  75.0 32.1 reduce-scatter.14
  110.3 34.1 reduce-scatter.12
  147.3 19.2 reduce-scatter.10
  168.7 17.4 reduce-scatter.8
